TPU v7x, 32 devices: a whole 2x2x4 slice. The times are simulated.
32 devices in a mesh: dp: 4 (over x, core), row: 4 (over z), col: 2 (over y).
Axes of the slice: x: 2, y: 2, z: 4, core: 2. Of those that a mesh axis runs over, the one named last changes fastest.
Arguments:
- hidden_in: float32 [1024, 32768], P('col', ('dp', 'row')), may hold values from -6 to 6
- lengths: int32 [64], P(('dp', 'row')), may hold values from 1 to 512, as said below
- ln1_gain: float32 [1024], P('col'), may hold values from 0.25 to 1.75
- ln1_shift: float32 [1024], P('col'), may hold values from -3 to 3
- w_qkv: bfloat16 [1024, 3072], P('row', 'col'), may hold values from -0.1875 to 0.1875
- bias_q: float32 [1024], P('col'), may hold values from -3 to 3
- bias_v: float32 [1024], P('col'), may hold values from -3 to 3
- w_out: bfloat16 [1024, 1024], P('col', 'row'), may hold values from -0.375 to 0.375
- bias_out: float32 [1024], P('col'), may hold values from -3 to 3
- ln2_gain: float32 [1024], P('col'), may hold values from 0.25 to 1.75
- ln2_shift: float32 [1024], P('col'), may hold values from -3 to 3
- w_up: bfloat16 [1024, 4096], P('row', 'col'), may hold values from -0.1875 to 0.1875
- bias_up: float32 [4096], P('col'), may hold values from -3 to 3
- w_down: bfloat16 [4096, 1024], P('col', 'row'), may hold values from -0.125 to 0.125
- bias_down: float32 [1024], P('col'), may hold values from -3 to 3
- cotangent: float32 [1024, 32768], P('col', ('dp', 'row')), may hold values from -6 to 6
Outputs:
- hidden_out: float32 [1024, 32768], P('col', ('dp', 'row'))
- grad_in: float32 [1024, 32768], P('col', ('dp', 'row'))
- grad_ln1_gain: float32 [1024], P('col')
- grad_ln1_shift: float32 [1024], P('col')
- grad_w_qkv: float32 [1024, 3072], P('row', 'col')
- grad_bias_q: float32 [1024], P('col')
- grad_bias_v: float32 [1024], P('col')
- grad_w_out: float32 [1024, 1024], P('col', 'row')
- grad_bias_out: float32 [1024], P('col')
- grad_ln2_gain: float32 [1024], P('col')
- grad_ln2_shift: float32 [1024], P('col')
- grad_w_up: float32 [1024, 4096], P('row', 'col')
- grad_bias_up: float32 [4096], P('col')
- grad_w_down: float32 [4096, 1024], P('col', 'row')
- grad_bias_down: float32 [1024], P('col')
Inputs may be any that keep to these rules, and one draw needn't show every extreme that they name: `lengths`: each slot holds one sequence of this many tokens followed by padding; some slot of every index pair of dp and row is full.
All inputs are finite; a program needn't handle non-finite values.
Results may differ from a plain program's by a relative error of at most 0.019.
Values may be sent and summed in bfloat16 or wider, within the bound.
A program may use at most 192 MiB of HBM per device.

v0:
```python
from functools import partial
import jax
import jax.numpy as jnp
from jax import lax
from jax.sharding import PartitionSpec as P

HEADS = 16
HEAD = 64
EPS = 1e-05
NEG = -1e30


def norm_forward(value, gain, shift):
    width = value.shape[1] * lax.axis_size("col")
    sums = lax.psum((jnp.sum(value, axis=1), jnp.sum(value * value, axis=1)), "col")
    mean = (sums[0] / width)[:, None]
    var = (sums[1] / width)[:, None] - mean * mean
    inverse = lax.rsqrt(var + EPS)
    normed = (value - mean) * inverse
    return (normed, inverse, (normed * gain + shift).astype(jnp.bfloat16))


def norm_backward(incoming, normed, inverse, gain):
    width = incoming.shape[1] * lax.axis_size("col")
    scaled = incoming * gain
    sums = lax.psum((jnp.sum(scaled, axis=1), jnp.sum(scaled * normed, axis=1)), "col")
    return inverse * (scaled - sums[0][:, None] / width - normed * sums[1][:, None] / width)


def gather_rows(value):
    return lax.all_gather(value, "col", axis=1, tiled=True)


def back_columns(value):
    return lax.psum_scatter(
        value.astype(jnp.bfloat16), "col", scatter_dimension=1, tiled=True
    ).astype(jnp.float32)


def slot_scores(slopes, query, keys, length):
    span = query.shape[0]
    pos = jnp.arange(span)
    offset = (pos[None, :] - pos[:, None]).astype(jnp.float32)
    raw = jnp.einsum("qhd,khd->hqk", query, keys, preferred_element_type=jnp.float32) * 0.125
    raw = raw + slopes[:, None, None] * offset[None]
    visible = (pos[None, :] <= pos[:, None]) & (pos[None, :] < length)
    return jnp.where(visible[None], raw, NEG)


def forward_slot(slopes, item):
    query, keys, values, length = item
    scores = slot_scores(slopes, query, keys, length)
    top = jnp.max(scores, axis=-1, keepdims=True)
    expo = jnp.exp(scores - top)
    total = jnp.sum(expo, axis=-1, keepdims=True)
    probs = expo / total
    attended = jnp.einsum(
        "hqk,khd->qhd", probs.astype(jnp.bfloat16), values, preferred_element_type=jnp.float32
    )
    return (attended, (top + jnp.log(total))[..., 0])


def backward_slot(slopes, item):
    query, keys, values, grad_out, lse, length = item
    scores = slot_scores(slopes, query, keys, length)
    probs = jnp.exp(scores - lse[..., None])
    grad_probs = jnp.einsum("qhd,khd->hqk", grad_out, values, preferred_element_type=jnp.float32)
    grad_values = jnp.einsum(
        "hqk,qhd->khd", probs.astype(jnp.bfloat16), grad_out, preferred_element_type=jnp.float32
    )
    inner = jnp.sum(probs * grad_probs, axis=-1, keepdims=True)
    grad_scores = (probs * (grad_probs - inner)).astype(jnp.bfloat16)
    grad_query = (
        jnp.einsum("hqk,khd->qhd", grad_scores, keys, preferred_element_type=jnp.float32) * 0.125
    )
    grad_keys = (
        jnp.einsum("hqk,qhd->khd", grad_scores, query, preferred_element_type=jnp.float32) * 0.125
    )
    return (grad_query, grad_keys, grad_values)


def body(
    hidden_in,
    lengths,
    ln1_gain,
    ln1_shift,
    w_qkv,
    bias_q,
    bias_v,
    w_out,
    bias_out,
    ln2_gain,
    ln2_shift,
    w_up,
    bias_up,
    w_down,
    bias_down,
    cotangent,
):
    tokens_in = jnp.transpose(hidden_in)
    grad_given = jnp.transpose(cotangent)
    rows = tokens_in.shape[0]
    slots = lengths.shape[0]
    span = rows // slots
    heads_here = w_qkv.shape[1] // (3 * HEAD)
    head_ids = lax.axis_index("col") * heads_here + jnp.arange(heads_here)
    slopes = jnp.exp2(-8.0 * (head_ids.astype(jnp.float32) + 1.0) / HEADS)
    qkv_full, up_full, out_full, down_full = (
        lax.all_gather(w_qkv, "row", axis=0, tiled=True),
        lax.all_gather(w_up, "row", axis=0, tiled=True),
        lax.all_gather(w_out, "row", axis=1, tiled=True),
        lax.all_gather(w_down, "row", axis=1, tiled=True),
    )
    normed1, inverse1, low1 = norm_forward(tokens_in, ln1_gain, ln1_shift)
    rows1 = gather_rows(low1)
    mixed = jnp.dot(rows1, qkv_full, preferred_element_type=jnp.float32).reshape(
        rows, heads_here, 3, HEAD
    )
    query = (
        (mixed[:, :, 0] + bias_q.reshape(heads_here, HEAD))
        .astype(jnp.bfloat16)
        .reshape(slots, span, heads_here, HEAD)
    )
    keys = mixed[:, :, 1].astype(jnp.bfloat16).reshape(slots, span, heads_here, HEAD)
    values = (
        (mixed[:, :, 2] + bias_v.reshape(heads_here, HEAD))
        .astype(jnp.bfloat16)
        .reshape(slots, span, heads_here, HEAD)
    )
    attended, lse = lax.map(partial(forward_slot, slopes), (query, keys, values, lengths))
    attn_low = attended.reshape(rows, heads_here * HEAD).astype(jnp.bfloat16)
    projected = lax.psum_scatter(
        jnp.dot(attn_low, out_full, preferred_element_type=jnp.float32),
        "col",
        scatter_dimension=1,
        tiled=True,
    )
    hidden1 = tokens_in + projected + bias_out
    normed2, inverse2, low2 = norm_forward(hidden1, ln2_gain, ln2_shift)
    rows2 = gather_rows(low2)
    pre = jnp.dot(rows2, up_full, preferred_element_type=jnp.float32) + bias_up
    act, act_pull = jax.vjp(partial(jax.nn.gelu, approximate=True), pre)
    act_low = act.astype(jnp.bfloat16)
    down_terms = jnp.dot(act_low, down_full, preferred_element_type=jnp.float32)
    result = (
        hidden1
        + lax.psum_scatter(
            down_terms.astype(jnp.bfloat16), "col", scatter_dimension=1, tiled=True
        ).astype(jnp.float32)
        + bias_down
    )
    grad_low = grad_given.astype(jnp.bfloat16)
    grad_full = lax.all_gather(grad_low, "col", axis=1, tiled=True)
    grad_down = jnp.einsum("tf,td->fd", act_low, grad_full, preferred_element_type=jnp.float32)
    grad_act = jnp.einsum("td,fd->tf", grad_full, down_full, preferred_element_type=jnp.float32)
    grad_pre = act_pull(grad_act)[0]
    grad_pre_low = grad_pre.astype(jnp.bfloat16)
    grad_up = jnp.einsum("td,tf->df", rows2, grad_pre_low, preferred_element_type=jnp.float32)
    grad_norm2 = back_columns(
        jnp.einsum("tf,df->td", grad_pre_low, up_full, preferred_element_type=jnp.float32)
    )
    grad_hidden1 = grad_given + norm_backward(grad_norm2, normed2, inverse2, ln2_gain)
    branch_low = grad_hidden1.astype(jnp.bfloat16)
    grad_branch = lax.all_gather(branch_low, "col", axis=1, tiled=True)
    grad_outw = jnp.einsum("tc,td->cd", attn_low, grad_branch, preferred_element_type=jnp.float32)
    grad_attn = jnp.einsum(
        "td,cd->tc", grad_branch, out_full, preferred_element_type=jnp.float32
    ).astype(jnp.bfloat16)
    grad_attn = grad_attn.reshape(slots, span, heads_here, HEAD)
    grad_query, grad_keys, grad_values = lax.map(
        partial(backward_slot, slopes), (query, keys, values, grad_attn, lse, lengths)
    )
    stacked = jnp.stack((grad_query, grad_keys, grad_values), axis=3).reshape(
        rows, 3 * heads_here * HEAD
    )
    stacked_low = stacked.astype(jnp.bfloat16)
    grad_qkv = jnp.einsum("td,tc->dc", rows1, stacked_low, preferred_element_type=jnp.float32)
    grad_norm1 = back_columns(
        jnp.einsum("tc,dc->td", stacked_low, qkv_full, preferred_element_type=jnp.float32)
    )
    grad_input = grad_hidden1 + norm_backward(grad_norm1, normed1, inverse1, ln1_gain)
    small = lax.psum(
        (
            jnp.sum(grad_norm1 * normed1, axis=0),
            jnp.sum(grad_norm1, axis=0),
            jnp.sum(grad_query.reshape(rows, heads_here * HEAD), axis=0),
            jnp.sum(grad_values.reshape(rows, heads_here * HEAD), axis=0),
            jnp.sum(grad_hidden1, axis=0),
            jnp.sum(grad_norm2 * normed2, axis=0),
            jnp.sum(grad_norm2, axis=0),
            jnp.sum(grad_pre, axis=0),
            jnp.sum(grad_given, axis=0),
        ),
        ("dp", "row"),
    )
    local = (grad_qkv, grad_up, grad_outw, grad_down)
    whole = (
        lax.psum(local[0].astype(jnp.bfloat16), "dp").astype(jnp.float32),
        lax.psum(local[1].astype(jnp.bfloat16), "dp").astype(jnp.float32),
        lax.psum(local[2].astype(jnp.bfloat16), "dp").astype(jnp.float32),
        lax.psum(local[3].astype(jnp.bfloat16), "dp").astype(jnp.float32),
    )
    summed = (
        lax.psum_scatter(
            whole[0].astype(jnp.bfloat16), "row", scatter_dimension=0, tiled=True
        ).astype(jnp.float32),
        lax.psum_scatter(
            whole[1].astype(jnp.bfloat16), "row", scatter_dimension=0, tiled=True
        ).astype(jnp.float32),
        lax.psum_scatter(
            whole[2].astype(jnp.bfloat16), "row", scatter_dimension=1, tiled=True
        ).astype(jnp.float32),
        lax.psum_scatter(
            whole[3].astype(jnp.bfloat16), "row", scatter_dimension=1, tiled=True
        ).astype(jnp.float32),
    )
    return (
        jnp.transpose(result),
        jnp.transpose(grad_input),
        small[0],
        small[1],
        summed[0],
        small[2],
        small[3],
        summed[2],
        small[4],
        small[5],
        small[6],
        summed[1],
        small[7],
        summed[3],
        small[8],
    )


def solution(mesh):
    return jax.shard_map(
        body,
        mesh=mesh,
        in_specs=(
            P("col", ("dp", "row")),
            P(("dp", "row")),
            P("col"),
            P("col"),
            P("row", "col"),
            P("col"),
            P("col"),
            P("col", "row"),
            P("col"),
            P("col"),
            P("col"),
            P("row", "col"),
            P("col"),
            P("col", "row"),
            P("col"),
            P("col", ("dp", "row")),
        ),
        out_specs=(
            P("col", ("dp", "row")),
            P("col", ("dp", "row")),
            P("col"),
            P("col"),
            P("row", "col"),
            P("col"),
            P("col"),
            P("col", "row"),
            P("col"),
            P("col"),
            P("col"),
            P("row", "col"),
            P("col"),
            P("col", "row"),
            P("col"),
        ),
        check_vma=False,
    )
```

profile of v0, /device:TPU:0, one launch (start us, length us, event | category | flops | bytes accessed | tf_op | source)
XLA Modules:
  0.0 1329.2 jit_solution(10266186835196599832)
XLA Ops:
  17.6 9.6 all-reduce.4
  34.8 53.8 %all-gather.9.cloned.1.call-done = bf16[2048,1024]{1,0:T(8,128)(2,1)} async-done(((bf16[2048,512]{1,0:T(8,128)(2,1)}), bf16[2048,1024]{1,0:T(8,128)(2,1)}) %all-gather.9.cloned.1.call-update) | async-done | bytes 4194320 | tf_op jit(solution)/shard_map/all_gather | solution.py:31
  88.6 65.1 %all-gather.11.cloned.1.call-done = bf16[1024,1536]{1,0:T(8,128)(2,1)} async-done(((bf16[256,1536]{1,0:T(8,128)(2,1)}), bf16[1024,1536]{1,0:T(8,128)(2,1)}) %all-gather.11.cloned.1.call-update) | async-done | bytes 3145744 | tf_op jit(solution)/shard_map/all_gather | solution.py:109
  153.7 9.8 fusion.100
  198.4 53.5 %while.30 = (s32[]{:T(128)}, bf16[4,512,8,64]{1,3,2,0:T(8,128)(2,1)}, f32[4,8,512]{2,1,0:T(8,128)}, bf16[4,512,8,64]{1,3,2,0:T(8,128)(2,1)}, s32[4]{0:T(128)S(1)...) while((s32[]{:T(128)}, ...), condition=%wide.region_7.8_spmd.clone.clone, body=%wide.region_4.7_spmd.clone.sunk.clone | while | flops 575664640 | bytes 49942764 | solution.py:130
  266.0 97.4 %reduce-scatter.9.cloned.1.call-done = f32[2048,512]{1,0:T(8,128)} async-done(((f32[2048,1024]{1,0:T(8,128)}), f32[2048,512]{1,0:T(8,128)}) %reduce-scatter.9.cloned.1.call-update) | async-done | bytes 4194320 | tf_op jit(solution)/shard_map/reduce_scatter | solution.py:132
  390.2 55.4 %all-gather.17.cloned.1.call-done = bf16[1024,2048]{1,0:T(8,128)(2,1)} async-done(((bf16[256,2048]{1,0:T(8,128)(2,1)}), bf16[1024,2048]{1,0:T(8,128)(2,1)}) %all-gather.17.cloned.1.call-update) | async-done | bytes 4194320 | tf_op jit(solution)/shard_map/all_gather | solution.py:110
  445.6 56.8 %all-gather.15.cloned.1.call-done = bf16[2048,1024]{1,0:T(8,128)(2,1)} async-done(((bf16[2048,512]{1,0:T(8,128)(2,1)}), bf16[2048,1024]{1,0:T(8,128)(2,1)}) %all-gather.15.cloned.1.call-update) | async-done | bytes 4194320 | tf_op jit(solution)/shard_map/all_gather | solution.py:31
  502.4 15.3 %fusion.102 = f32[2048,2048]{1,0:T(8,128)} fusion(bf16[2048,1024]{1,0:T(8,128)(2,1)} %all-gather.15.cloned.1.call-done, bf16[1024,2048]{1,0:T(8,128)(2,1)} %all-gather.17.cloned.1.call-done), kind=kOutput, calls=%fused_computation.144 | convolution fusion | flops 8589934592 | bytes 25165824 | tf_op jit(solution)/shard_map/dot_general | solution.py:141
  517.7 43.1 %all-gather.21.cloned.1.call-done = bf16[2048,1024]{1,0:T(8,128)(2,1)} async-done(((bf16[2048,512]{1,0:T(8,128)(2,1)}), bf16[2048,1024]{1,0:T(8,128)(2,1)}) %all-gather.21.cloned.1.call-update) | async-done | bytes 4194320 | tf_op jit(solution)/shard_map/all_gather | solution.py:153
  560.8 82.2 %all-gather.19.cloned.1.call-done = bf16[2048,1024]{1,0:T(8,128)(2,1)} async-done(((bf16[2048,256]{1,0:T(8,128)(2,1)}), bf16[2048,1024]{1,0:T(8,128)(2,1)}) %all-gather.19.cloned.1.call-update) | async-done | bytes 4194320 | tf_op jit(solution)/shard_map/all_gather | solution.py:112
  643.0 27.5 %fusion.91 = (f32[2048]{0:T(1024)}, bf16[2048,2048]{1,0:T(8,128)(2,1)}, bf16[2048,2048]{1,0:T(8,128)(2,1)}) fusion(f32[2048,2048]{1,0:T(8,128)} %fusion.102, f32[2048]{0:T(1024)S(1)} %copy-done.34, bf16[2048,1024]{1,0:T(8,128)(2,1)} %all-gather.21.cloned.1.call-done, bf16[2048,1024]{1,0:T(8,128)(2,1)} %all-gather.19.cloned.1.call-done), kind=kOutput, calls=%fused_computation.136 | convolution fusion | flops 8690595840 | bytes 41959424 | tf_op jit(solution)/shard_map/td,fd->tf/dot_general | solution.py:155
  670.5 13.0 fusion.84
  683.6 13.8 %convolution_convert_fusion.2 = bf16[2048,1024]{1,0:T(8,128)(2,1)} fusion(bf16[2048,2048]{1,0:T(8,128)(2,1)} %get-tuple-element.304, bf16[2048,1024]{1,0:T(8,128)(2,1)} %all-gather.19.cloned.1.call-done), kind=kOutput, calls=%fused_computation.122 | convolution fusion | flops 8592031744 | bytes 16777216 | tf_op jit(solution)/shard_map/dot_general | solution.py:144
  697.4 38.7 %reduce-scatter.13.cloned.1.call-done = bf16[2048,512]{1,0:T(8,128)(2,1)} async-done(((bf16[2048,1024]{1,0:T(8,128)(2,1)}), bf16[2048,512]{1,0:T(8,128)(2,1)}) %reduce-scatter.13.cloned.1.call-update) | async-done | bytes 2097168 | tf_op jit(solution)/shard_map/reduce_scatter | solution.py:35
  747.9 44.8 %reduce-scatter.11.cloned.1.call-done = bf16[2048,512]{1,0:T(8,128)(2,1)} async-done(((bf16[2048,1024]{1,0:T(8,128)(2,1)}), bf16[2048,512]{1,0:T(8,128)(2,1)}) %reduce-scatter.11.cloned.1.call-update) | async-done | bytes 2097168 | tf_op jit(solution)/shard_map/reduce_scatter | solution.py:147
  792.8 8.2 fusion.93
  804.6 14.2 %convolution_convert_fusion.3 = bf16[2048,1024]{1,0:T(8,128)(2,1)} fusion(bf16[2048,2048]{1,0:T(8,128)(2,1)} %get-tuple-element.304, bf16[2048,1024]{1,0:T(8,128)(2,1)} %all-gather.21.cloned.1.call-done), kind=kOutput, calls=%fused_computation.123 | convolution fusion | flops 8592031744 | bytes 16777216 | tf_op jit(solution)/shard_map/tf,td->fd/dot_general | solution.py:154
  818.8 14.1 %fusion.87 = bf16[1024,2048]{1,0:T(8,128)(2,1)} fusion(bf16[2048,1024]{1,0:T(8,128)(2,1)} %all-gather.15.cloned.1.call-done, bf16[2048,2048]{1,0:T(8,128)(2,1)} %get-tuple-element.296), kind=kOutput, calls=%fused_computation.121 | convolution fusion | flops 8592031744 | bytes 16777216 | tf_op jit(solution)/shard_map/td,tf->df/dot_general | solution.py:158
  833.0 28.5 %all-gather.23.cloned.1.call-done = bf16[2048,1024]{1,0:T(8,128)(2,1)} async-done(((bf16[2048,512]{1,0:T(8,128)(2,1)}), bf16[2048,1024]{1,0:T(8,128)(2,1)}) %all-gather.23.cloned.1.call-update) | async-done | bytes 4194320 | tf_op jit(solution)/shard_map/all_gather | solution.py:164
  880.7 133.4 %while.31 = (s32[]{:T(128)}, f32[4,512,8,64]{1,3,2,0:T(8,128)}, bf16[4,512,8,64]{1,3,2,0:T(8,128)(2,1)}, f32[4,512,8,64]{1,3,2,0:T(8,128)}, bf16[4,512,8,64]{1,3...) while((s32[]{:T(128)}, f32[4,512,8,64]{1,3,2,0:T(8,128)}, ...), condition=%wide.region_21.22_spmd.clone.clone, body=%wide.region_19.21_spmd.clone.sunk.clone | while | flops 1366815232 | bytes 122771752 | solution.py:170
  885.3 8.9 multiply_reduce_fusion.4
  918.7 8.9 multiply_reduce_fusion.4
  952.0 8.9 multiply_reduce_fusion.4
  985.3 8.9 multiply_reduce_fusion.4
  1022.4 8.3 copy.58
  1039.0 8.4 convolution_convert_fusion
  1050.7 61.7 %reduce-scatter.17.cloned.1.call-done = bf16[256,1536]{1,0:T(8,128)(2,1)} async-done(((bf16[1024,1536]{1,0:T(8,128)(2,1)}), bf16[256,1536]{1,0:T(8,128)(2,1)}) %reduce-scatter.17.cloned.1.call-update) | async-done | bytes 786448 | tf_op jit(solution)/shard_map/reduce_scatter | solution.py:204
  1112.4 11.7 convolution_convert_fusion.1
  1132.2 51.7 %all-reduce.8.cloned.1.call-done = (bf16[256,1536]{1,0:T(8,128)(2,1)}, bf16[512,256]{1,0:T(8,128)(2,1)}, bf16[256,2048]{1,0:T(8,128)(2,1)}, bf16[2048,256]{1,0:T(8,128)(2,1)}) async-done(((bf16[256,1536]{1,0:T(8,128)(2,1)}, bf16[512,256]{1,0:T(8,128)(2,1)}, bf16[256,2048]{1,0:T(8,128)(2,1)}, bf16[2048,256]{1,0:T(8,128)(2,1)}), (bf16[256,1536]{1,0:T(8,128)(2,1)}, bf16[512,256]{1,0:T(8,128)(2,1)}, ...) | async-done | bytes 3145744 | tf_op jit(solution)/shard_map/psum | solution.py:198
  1192.5 47.9 %reduce-scatter.15.cloned.1.call-done = bf16[2048,512]{1,0:T(8,128)(2,1)} async-done(((bf16[2048,1024]{1,0:T(8,128)(2,1)}), bf16[2048,512]{1,0:T(8,128)(2,1)}) %reduce-scatter.15.cloned.1.call-update) | async-done | bytes 2097168 | tf_op jit(solution)/shard_map/reduce_scatter | solution.py:35
  1262.6 59.9 %all-reduce = (f32[512]{0:T(512)}, f32[512]{0:T(512)}, f32[512]{0:T(512)}, f32[512]{0:T(512)}, f32[512]{0:T(512)}, /*index=5*/f32[512]{0:T(512)}, f32[512]{0:T(512)}, f32[2048]{0:T(1024)}, f32[512]{0:T(512)}) all-reduce(f32[512]{0:T(512)S(1)} %get-tuple-element.228, ...), channel_id=1, replica_groups=mesh['dp'=4,'row'=4,'col'=2] {'dp','row'}, use_global_device_ids=true, to_apply=%region_28.29 | all-reduce | flops 6144 | bytes 49152 | tf_op jit(solution)/shard_map/psum | solution.py:182
  (278 shorter events, 337.5 us)
Async XLA Ops:
  7.2 81.4 %all-gather.9.cloned.1.call-start = ((), (), s32[]{:S(2)}) async-start(), calls=%async_computation.8 | async-start | bytes 6291456 | tf_op jit(solution)/shard_map/all_gather | solution.py:31
  12.6 15.2 %copy-start.19 = (f32[512]{0:T(512)S(1)}, f32[512]{0:T(512)}, u32[]{:S(2)}) copy-start(f32[512]{0:T(512)} %param.22) | copy-start | bytes 6148
  12.6 15.2 %copy-start.25 = (f32[512]{0:T(512)S(1)}, f32[512]{0:T(512)}, u32[]{:S(2)}) copy-start(f32[512]{0:T(512)} %param.23) | copy-start | bytes 6148
  31.4 122.2 %all-gather.11.cloned.1.call-start = ((), (), s32[]{:S(2)}) async-start(), calls=%async_computation.9 | async-start | bytes 3932160 | tf_op jit(solution)/shard_map/all_gather | solution.py:109
  32.2 225.6 %all-gather.13.cloned.1.call-start = ((), (), s32[]{:S(2)}) async-start(), calls=%async_computation.10 | async-start | bytes 1310720 | tf_op jit(solution)/shard_map/all_gather | solution.py:111
  32.9 330.4 %reduce-scatter.9.cloned.1.call-start = ((), (), s32[]{:S(2)}) async-start(), calls=%async_computation.11 | async-start | bytes 12582912 | tf_op jit(solution)/shard_map/reduce_scatter | solution.py:132
  33.2 130.3 %copy-start.3 = (bf16[4,512,8,64]{1,3,2,0:T(8,128)(2,1)}, bf16[4,512,8,64]{1,3,2,0:T(8,128)(2,1)S(1)}, u32[]{:S(2)}) copy-start(bf16[4,512,8,64]{1,3,2,0:T(8,128)(2,1)S(1)} %fusion.99) | copy-start | bytes 6291460
  265.3 98.1 %copy-start.30 = (f32[512]{0:T(512)S(1)}, f32[512]{0:T(512)}, u32[]{:S(2)}) copy-start(f32[512]{0:T(512)} %param.28) | copy-start | bytes 6148
  265.3 180.3 %all-gather.17.cloned.1.call-start = ((), (), s32[]{:S(2)}) async-start(), calls=%async_computation.13 | async-start | bytes 5242880 | tf_op jit(solution)/shard_map/all_gather | solution.py:110
  265.9 110.3 %copy-start.18 = (f32[512]{0:T(512)S(1)}, f32[512]{0:T(512)}, u32[]{:S(2)}) copy-start(f32[512]{0:T(512)} %param.29) | copy-start | bytes 6148
  265.9 110.3 %copy-start.26 = (f32[512]{0:T(512)S(1)}, f32[512]{0:T(512)}, u32[]{:S(2)}) copy-start(f32[512]{0:T(512)} %param.30) | copy-start | bytes 6148
  265.9 236.5 %all-gather.15.cloned.1.call-start = ((), (), s32[]{:S(2)}) async-start(), calls=%async_computation.12 | async-start | bytes 6291456 | tf_op jit(solution)/shard_map/all_gather | solution.py:31
  379.9 180.9 %all-gather.21.cloned.1.call-start = ((), (), s32[]{:S(2)}) async-start(), calls=%async_computation.16 | async-start | bytes 6291456 | tf_op jit(solution)/shard_map/all_gather | solution.py:153
  389.4 253.6 %all-gather.19.cloned.1.call-start = ((), (), s32[]{:S(2)}) async-start(), calls=%async_computation.14 | async-start | bytes 5242880 | tf_op jit(solution)/shard_map/all_gather | solution.py:112
  390.2 252.9 %copy-start.34 = (f32[2048]{0:T(1024)S(1)}, f32[2048]{0:T(1024)}, u32[]{:S(2)}) copy-start(f32[2048]{0:T(1024)} %param.32) | copy-start | bytes 24580
  390.2 346.0 %reduce-scatter.13.cloned.1.call-start = ((), (), s32[]{:S(2)}) async-start(), calls=%async_computation.17 | async-start | bytes 6291456 | tf_op jit(solution)/shard_map/reduce_scatter | solution.py:35
  643.0 27.5 %copy-start.32 = (bf16[1024,2048]{1,0:T(8,128)(2,1)S(1)}, bf16[1024,2048]{1,0:T(8,128)(2,1)}, u32[]{:S(2)}) copy-start(bf16[1024,2048]{1,0:T(8,128)(2,1)} %all-gather.17.cloned.1.call-done) | copy-start | bytes 12582916
  683.5 109.2 %reduce-scatter.11.cloned.1.call-start = ((), (), s32[]{:S(2)}) async-start(), calls=%async_computation.15 | async-start | bytes 6291456 | tf_op jit(solution)/shard_map/reduce_scatter | solution.py:147
  697.4 95.4 %copy-start.27 = (f32[512]{0:T(512)S(1)}, f32[512]{0:T(512)}, u32[]{:S(2)}) copy-start(f32[512]{0:T(512)} %param.34) | copy-start | bytes 6148
  697.4 164.1 %all-gather.23.cloned.1.call-start = ((), (), s32[]{:S(2)}) async-start(), calls=%async_computation.18 | async-start | bytes 6291456 | tf_op jit(solution)/shard_map/all_gather | solution.py:164
  736.2 56.6 %copy-start.7 = (bf16[2048,512]{1,0:T(8,128)(2,1)S(1)}, bf16[2048,512]{1,0:T(8,128)(2,1)}, u32[]{:S(2)}) copy-start(bf16[2048,512]{1,0:T(8,128)(2,1)} %reduce-scatter.13.cloned.1.call-done) | copy-start | bytes 6291460
  804.5 242.9 %reduce-scatter.23.cloned.1.call-start = ((), (), s32[]{:S(2)}) async-start(), calls=%async_computation.23 | async-start | bytes 5242880 | tf_op jit(solution)/shard_map/reduce_scatter | solution.py:213
  818.8 228.7 %reduce-scatter.21.cloned.1.call-start = ((), (), s32[]{:S(2)}) async-start(), calls=%async_computation.22 | async-start | bytes 5242880 | tf_op jit(solution)/shard_map/reduce_scatter | solution.py:207
  832.9 28.6 %copy-start.33 = (bf16[512,1024]{1,0:T(8,128)(2,1)S(1)}, bf16[512,1024]{1,0:T(8,128)(2,1)}, u32[]{:S(2)}) copy-start(bf16[512,1024]{1,0:T(8,128)(2,1)} %all-gather.13.cloned.1.call-done) | copy-start | bytes 3145732
  832.9 217.7 %reduce-scatter.19.cloned.1.call-start = ((), (), s32[]{:S(2)}) async-start(), calls=%async_computation.21 | async-start | bytes 1310720 | tf_op jit(solution)/shard_map/reduce_scatter | solution.py:210
  1014.1 98.2 %reduce-scatter.17.cloned.1.call-start = ((), (), s32[]{:S(2)}) async-start(), calls=%async_computation.20 | async-start | bytes 3932160 | tf_op jit(solution)/shard_map/reduce_scatter | solution.py:204
  1047.4 136.4 %all-reduce.8.cloned.1.call-start = ((), (), s32[]{:S(2)}) async-start(), calls=%async_computation.24 | async-start | bytes 6291456 | tf_op jit(solution)/shard_map/psum | solution.py:198
  1112.4 128.0 %reduce-scatter.15.cloned.1.call-start = ((), (), s32[]{:S(2)}) async-start(), calls=%async_computation.19 | async-start | bytes 6291456 | tf_op jit(solution)/shard_map/reduce_scatter | solution.py:35
  1185.7 54.7 %copy-start.15 = (f32[2048]{0:T(1024)S(1)}, f32[2048]{0:T(1024)}, u32[]{:S(2)}) copy-start(f32[2048]{0:T(1024)} %copy-done.14) | copy-start | bytes 24580
  1185.7 54.7 %copy-start.17 = (f32[2048]{0:T(1024)S(1)}, f32[2048]{0:T(1024)}, u32[]{:S(2)}) copy-start(f32[2048]{0:T(1024)} %copy-done.16) | copy-start | bytes 24580
  1185.7 54.7 %copy-start.20 = (f32[512]{0:T(512)S(1)}, f32[512]{0:T(512)}, u32[]{:S(2)}) copy-start(f32[512]{0:T(512)} %param.22) | copy-start | bytes 6148
  1240.4 11.2 copy-start.8
  (37 other events, 166.0 us)
Sparse Core Ops, SparseCore 0:
  31.5 56.9 all-gather.8
  90.1 63.4 all-gather.10
  155.2 28.8 all-gather.12
  265.4 97.8 reduce-scatter.8
  364.8 80.7 all-gather.16
  447.1 55.2 all-gather.14
  504.0 56.7 all-gather.20
  562.4 80.5 all-gather.18
  683.6 52.4 reduce-scatter.12
  738.3 54.3 reduce-scatter.10
  804.7 56.8 all-gather.22
  863.8 76.7 reduce-scatter.22
  942.8 77.3 reduce-scatter.20
  1023.0 27.6 reduce-scatter.18
  1053.4 58.8 reduce-scatter.16
  1114.8 68.9 all-reduce.7
  1186.0 54.3 reduce-scatter.14
where the time goes:
time: 1340 us; the launch traced here: 1330 us
  waiting for transfers between devices  733 us (55%)
  matrix products  269 us (20%)
  other arithmetic  124 us (9%)
  local copies, waits for them, and re-layouts  96.6 us (7%)
  blocking collectives  90.2 us (7%)
  between operations  14.5 us (1%)
    all_gather x2, waiting for transfers between devices, gather_rows(): return lax.all_gather(value, 'col', axis=1, tiled=True)  111 us
    reduce_scatter x1, waiting for transfers between devices, body(): lax.psum_scatter(jnp.dot(attn_low, out_full, preferred_element_type=jnp.f...  97.4 us
    reduce_scatter x2, waiting for transfers between devices, back_columns(): lax.psum_scatter(value.astype(jnp.bfloat16), 'col', scatter_dimension=1,...  86.7 us
    all_gather x1, waiting for transfers between devices, body(): lax.all_gather(w_down, 'row', axis=1, tiled=True)  82.2 us
    all_gather x1, waiting for transfers between devices, body(): lax.all_gather(w_qkv, 'row', axis=0, tiled=True)  65.1 us
    reduce_scatter x1, waiting for transfers between devices, body(): lax.psum_scatter(whole[0].astype(jnp.bfloat16), 'row', scatter_dimension=...  61.7 us
    psum x1, blocking collectives, body(): lax.psum((jnp.sum(grad_norm1 * normed1, axis=0), jnp.sum(grad_norm1, axis...  59.9 us
    all_gather x1, waiting for transfers between devices, body(): lax.all_gather(w_up, 'row', axis=0, tiled=True)  55.4 us
  transfers between devices with their start and end apart: 17, of which 14 were waited for; matrix products, arithmetic and copies ran while one was open for 30% of the time, Pallas kernels for 0%

commit v1 on v0

--- a/solution.py
+++ b/solution.py
@@ -8,6 +8,13 @@
 HEAD = 64
 EPS = 1e-05
 NEG = -1e30
+
+
+def lift_files_by_axis(xs, in_dim):
+    xs = jnp.moveaxis(xs, 0, in_dim)
+    a_next = xs.shape
+    z = xs.reshape(*a_next[:in_dim], a_next[in_dim] * a_next[in_dim + 1], *a_next[in_dim + 2 :])
+    return z
 
 
 def norm_forward(value, gain, shift):
@@ -105,9 +112,28 @@
     heads_here = w_qkv.shape[1] // (3 * HEAD)
     head_ids = lax.axis_index("col") * heads_here + jnp.arange(heads_here)
     slopes = jnp.exp2(-8.0 * (head_ids.astype(jnp.float32) + 1.0) / HEADS)
+
+    def order_frame(inputs, axis_tag, dim_k):
+        dev_n = jax.lax.axis_size(axis_tag)
+        by_place = list(map(lambda ix: (ix, (ix + 1) % dev_n), range(dev_n)))
+        even, z2 = ([], [])
+        src_i = 0
+        windows = [(h, dd) for dd, h in by_place]
+        while src_i < dev_n - 1:
+            if src_i % 2 == 0:
+                even.append(jax.lax.ppermute(even[-1] if even else inputs, axis_tag, by_place))
+            else:
+                z2.append(jax.lax.ppermute(z2[-1] if z2 else inputs, axis_tag, windows))
+            src_i = src_i + 1
+        odd = jnp.stack([*even[::-1], inputs, *z2], 0)
+        arr_next = jax.lax.axis_index(axis_tag) - len(even)
+        odd = odd[(jnp.arange(dev_n) - arr_next) % dev_n]
+        clean = lift_files_by_axis(odd, dim_k)
+        return clean
+
     qkv_full, up_full, out_full, down_full = (
         lax.all_gather(w_qkv, "row", axis=0, tiled=True),
-        lax.all_gather(w_up, "row", axis=0, tiled=True),
+        order_frame(w_up, "row", 0),
         lax.all_gather(w_out, "row", axis=1, tiled=True),
         lax.all_gather(w_down, "row", axis=1, tiled=True),
     )

time: 1340 us -> 1260 us (0.940)
  waiting for transfers between devices: 733 us -> 650 us
    all_gather x1 -> x0, waiting for transfers between devices: 55.4 us -> none  [body(): lax.all_gather(w_up, 'row', axis=0, tiled=True)]
    ppermute x0 -> x3, waiting for transfers between devices: none -> 44 us  [the longest x1 23.6 us: order_frame(): z2.append(jax.lax.ppermute(z2[-1] if z2 else inputs, axis_tag, windows))]
    all_gather x1, waiting for transfers between devices: 43.1 us -> 0.01 us  [body(): grad_full = lax.all_gather(grad_low, 'col', axis=1, tiled=True)]
    all_gather x2, waiting for transfers between devices: 111 us -> 95.1 us  [gather_rows(): return lax.all_gather(value, 'col', axis=1, tiled=True)]
    all_gather x1, waiting for transfers between devices: 82.2 us -> 67.7 us  [body(): lax.all_gather(w_down, 'row', axis=1, tiled=True)]
    dot_general x4, matrix products: 23.9 us -> 9.69 us  [backward_slot(): jnp.einsum('hqk,qhd->khd', probs.astype(jnp.bfloat16), grad_out, preferre...]
    unnamed x76 -> x82, local copies, waits for them, and re-layouts: 47.8 us -> 51.1 us
  transfers between devices with their start and end apart: 17 -> 19, of which waited for: 14 -> 14; matrix products, arithmetic and copies ran while one was open for 30% -> 31% of each run, Pallas kernels for 0% -> 0%
where the time goes in v1:
time: 1260 us; the launch traced here: 1250 us
  waiting for transfers between devices  650 us (52%)
  matrix products  256 us (20%)
  other arithmetic  126 us (10%)
  local copies, waits for them, and re-layouts  108 us (9%)
  blocking collectives  90.4 us (7%)
  between operations  14.5 us (1%)
    all_gather x2, waiting for transfers between devices, gather_rows(): return lax.all_gather(value, 'col', axis=1, tiled=True)  95.1 us
    reduce_scatter x2, waiting for transfers between devices, back_columns(): lax.psum_scatter(value.astype(jnp.bfloat16), 'col', scatter_dimension=1,...  89.4 us
    reduce_scatter x1, waiting for transfers between devices, body(): lax.psum_scatter(jnp.dot(attn_low, out_full, preferred_element_type=jnp.f...  87.9 us
    all_gather x1, waiting for transfers between devices, body(): lax.all_gather(w_down, 'row', axis=1, tiled=True)  67.7 us
    all_gather x1, waiting for transfers between devices, body(): lax.all_gather(w_qkv, 'row', axis=0, tiled=True)  65.1 us
    reduce_scatter x1, waiting for transfers between devices, body(): lax.psum_scatter(whole[0].astype(jnp.bfloat16), 'row', scatter_dimension=...  61.7 us
    psum x1, blocking collectives, body(): lax.psum((jnp.sum(grad_norm1 * normed1, axis=0), jnp.sum(grad_norm1, axis...  59.9 us
    psum x1, waiting for transfers between devices, body(): lax.psum(local[0].astype(jnp.bfloat16), 'dp').astype(jnp.float32)  51.7 us
  transfers between devices with their start and end apart: 19, of which 14 were waited for; matrix products, arithmetic and copies ran while one was open for 31% of the time, Pallas kernels for 0%

profile of v1, /device:TPU:0, one launch (start us, length us, event | category | flops | bytes accessed | tf_op | source)
XLA Modules:
  0.0 1250.9 jit_solution(3859143876658172658)
XLA Ops:
  17.6 9.6 all-reduce.4
  34.8 53.8 %all-gather.8.cloned.1.call-done = bf16[2048,1024]{1,0:T(8,128)(2,1)} async-done(((bf16[2048,512]{1,0:T(8,128)(2,1)}), bf16[2048,1024]{1,0:T(8,128)(2,1)}) %all-gather.8.cloned.1.call-update) | async-done | bytes 4194320 | tf_op jit(solution)/shard_map/all_gather | solution.py:38
  88.6 65.1 %all-gather.10.cloned.1.call-done = bf16[1024,1536]{1,0:T(8,128)(2,1)} async-done(((bf16[256,1536]{1,0:T(8,128)(2,1)}), bf16[1024,1536]{1,0:T(8,128)(2,1)}) %all-gather.10.cloned.1.call-update) | async-done | bytes 3145744 | tf_op jit(solution)/shard_map/all_gather | solution.py:135
  153.7 9.8 fusion.102
  198.4 53.3 %while.30 = (s32[]{:T(128)}, bf16[4,512,8,64]{1,3,2,0:T(8,128)(2,1)}, f32[4,8,512]{2,1,0:T(8,128)}, bf16[4,512,8,64]{1,3,2,0:T(8,128)(2,1)}, s32[4]{0:T(128)S(1)...) while((s32[]{:T(128)}, ...), condition=%wide.region_7.8_spmd.clone.clone, body=%wide.region_4.7_spmd.clone.sunk.clone | while | flops 575664640 | bytes 33165512 | solution.py:156
  275.2 87.9 %reduce-scatter.9.cloned.1.call-done = f32[2048,512]{1,0:T(8,128)} async-done(((f32[2048,1024]{1,0:T(8,128)}), f32[2048,512]{1,0:T(8,128)}) %reduce-scatter.9.cloned.1.call-update) | async-done | bytes 4194320 | tf_op jit(solution)/shard_map/reduce_scatter | solution.py:158
  383.9 23.6 %collective-permute-done.2 = bf16[256,2048]{1,0:T(8,128)(2,1)S(1)} collective-permute-done((bf16[256,2048]{1,0:T(8,128)(2,1)S(1)}, bf16[256,2048]{1,0:T(8,128)(2,1)S(1)}, u32[]{:S(2)}, u32[]{:S(2)}) %collective-permute-start.2) | collective-permute-done | bytes 1048608 | tf_op jit(solution)/shard_map/ppermute | solution.py:126
  407.5 20.4 %collective-permute-done.1 = bf16[256,2048]{1,0:T(8,128)(2,1)} collective-permute-done((bf16[256,2048]{1,0:T(8,128)(2,1)S(1)}, bf16[256,2048]{1,0:T(8,128)(2,1)}, u32[]{:S(2)}, u32[]{:S(2)}) %collective-permute-start.1) | collective-permute-done | bytes 1048608 | tf_op jit(solution)/shard_map/ppermute | solution.py:124
  436.4 67.7 %all-gather.16.cloned.1.call-done = bf16[2048,1024]{1,0:T(8,128)(2,1)} async-done(((bf16[2048,256]{1,0:T(8,128)(2,1)}), bf16[2048,1024]{1,0:T(8,128)(2,1)}) %all-gather.16.cloned.1.call-update) | async-done | bytes 4194320 | tf_op jit(solution)/shard_map/all_gather | solution.py:138
  504.1 15.3 %fusion.104 = f32[2048,2048]{1,0:T(8,128)} fusion(bf16[2048,1024]{1,0:T(8,128)(2,1)} %all-gather.18.cloned.1.call-done, bf16[2048,1024]{1,0:T(8,128)(2,1)} %all-gather.16.cloned.1.call-done), kind=kOutput, calls=%fused_computation.153 | convolution fusion | flops 8589934592 | bytes 25165824 | tf_op jit(solution)/shard_map/td,fd->tf/dot_general | solution.py:181
  519.4 41.3 %all-gather.14.cloned.1.call-done = bf16[2048,1024]{1,0:T(8,128)(2,1)} async-done(((bf16[2048,512]{1,0:T(8,128)(2,1)}), bf16[2048,1024]{1,0:T(8,128)(2,1)}) %all-gather.14.cloned.1.call-update) | async-done | bytes 4194320 | tf_op jit(solution)/shard_map/all_gather | solution.py:38
  560.7 27.2 %fusion.93 = (f32[2048]{0:T(1024)}, bf16[2048,2048]{1,0:T(8,128)(2,1)S(1)}, bf16[2048,2048]{1,0:T(8,128)(2,1)}) fusion(f32[2048,2048]{1,0:T(8,128)} %fusion.104, f32[2048]{0:T(1024)S(1)} %copy-done.35, bf16[2048,1024]{1,0:T(8,128)(2,1)} %all-gather.14.cloned.1.call-done, bf16[1024,2048]{1,0:T(8,128)(2,1)} %bitcast.226), kind=kOutput, calls=%fused_computation.145 | convolution fusion | flops 8690595840 | bytes 41959424 | tf_op jit(solution)/shard_map/dot_general | solution.py:167
  591.2 11.2 fusion.84
  602.5 13.8 %convolution_convert_fusion.2 = bf16[2048,1024]{1,0:T(8,128)(2,1)} fusion(bf16[2048,2048]{1,0:T(8,128)(2,1)} %get-tuple-element.304, bf16[2048,1024]{1,0:T(8,128)(2,1)} %all-gather.16.cloned.1.call-done), kind=kOutput, calls=%fused_computation.124 | convolution fusion | flops 8592031744 | bytes 16777216 | tf_op jit(solution)/shard_map/dot_general | solution.py:170
  616.3 40.5 %reduce-scatter.13.cloned.1.call-done = bf16[2048,512]{1,0:T(8,128)(2,1)} async-done(((bf16[2048,1024]{1,0:T(8,128)(2,1)}), bf16[2048,512]{1,0:T(8,128)(2,1)}) %reduce-scatter.13.cloned.1.call-update) | async-done | bytes 2097168 | tf_op jit(solution)/shard_map/reduce_scatter | solution.py:42
  668.6 45.5 %reduce-scatter.11.cloned.1.call-done = bf16[2048,512]{1,0:T(8,128)(2,1)} async-done(((bf16[2048,1024]{1,0:T(8,128)(2,1)}), bf16[2048,512]{1,0:T(8,128)(2,1)}) %reduce-scatter.11.cloned.1.call-update) | async-done | bytes 2097168 | tf_op jit(solution)/shard_map/reduce_scatter | solution.py:173
  726.1 14.2 %fusion.87 = bf16[1024,2048]{1,0:T(8,128)(2,1)} fusion(bf16[2048,1024]{1,0:T(8,128)(2,1)} %all-gather.14.cloned.1.call-done, bf16[2048,2048]{1,0:T(8,128)(2,1)} %copy-done.38), kind=kOutput, calls=%fused_computation.123 | convolution fusion | flops 8592031744 | bytes 16777216 | tf_op jit(solution)/shard_map/td,tf->df/dot_general | solution.py:184
  740.4 14.0 %convolution_convert_fusion.3 = bf16[2048,1024]{1,0:T(8,128)(2,1)} fusion(bf16[2048,2048]{1,0:T(8,128)(2,1)} %get-tuple-element.304, bf16[2048,1024]{1,0:T(8,128)(2,1)} %all-gather.18.cloned.1.call-done), kind=kOutput, calls=%fused_computation.125 | convolution fusion | flops 8592031744 | bytes 16777216 | tf_op jit(solution)/shard_map/tf,td->fd/dot_general | solution.py:180
  754.5 28.5 %all-gather.20.cloned.1.call-done = bf16[2048,1024]{1,0:T(8,128)(2,1)} async-done(((bf16[2048,512]{1,0:T(8,128)(2,1)}), bf16[2048,1024]{1,0:T(8,128)(2,1)}) %all-gather.20.cloned.1.call-update) | async-done | bytes 4194320 | tf_op jit(solution)/shard_map/all_gather | solution.py:190
  802.2 125.7 %while.31 = (s32[]{:T(128)}, f32[4,512,8,64]{1,3,2,0:T(8,128)}, bf16[4,512,8,64]{1,3,2,0:T(8,128)(2,1)}, f32[4,512,8,64]{1,3,2,0:T(8,128)}, bf16[4,512,8,64]{1,3...) while((s32[]{:T(128)}, f32[4,512,8,64]{1,3,2,0:T(8,128)}, ...), condition=%wide.region_21.22_spmd.clone.clone, body=%wide.region_19.21_spmd.clone.sunk.clone | while | flops 1366815232 | bytes 156326224 | solution.py:196
  807.0 8.7 multiply_reduce_fusion.4
  838.4 8.7 multiply_reduce_fusion.4
  869.9 8.8 multiply_reduce_fusion.4
  901.3 8.7 multiply_reduce_fusion.4
  936.3 8.3 copy.58
  952.9 8.4 convolution_convert_fusion
  961.4 10.9 reduce-scatter.19.cloned.1.call-done
  972.3 61.7 %reduce-scatter.17.cloned.1.call-done = bf16[256,1536]{1,0:T(8,128)(2,1)} async-done(((bf16[1024,1536]{1,0:T(8,128)(2,1)}), bf16[256,1536]{1,0:T(8,128)(2,1)}) %reduce-scatter.17.cloned.1.call-update) | async-done | bytes 786448 | tf_op jit(solution)/shard_map/reduce_scatter | solution.py:230
  1034.0 11.7 convolution_convert_fusion.1
  1053.8 51.7 %all-reduce.8.cloned.1.call-done = (bf16[256,1536]{1,0:T(8,128)(2,1)}, bf16[512,256]{1,0:T(8,128)(2,1)}, bf16[256,2048]{1,0:T(8,128)(2,1)}, bf16[2048,256]{1,0:T(8,128)(2,1)}) async-done(((bf16[256,1536]{1,0:T(8,128)(2,1)}, bf16[512,256]{1,0:T(8,128)(2,1)}, bf16[256,2048]{1,0:T(8,128)(2,1)}, bf16[2048,256]{1,0:T(8,128)(2,1)}), (bf16[256,1536]{1,0:T(8,128)(2,1)}, bf16[512,256]{1,0:T(8,128)(2,1)}, ...) | async-done | bytes 3145744 | tf_op jit(solution)/shard_map/psum | solution.py:224
  1113.2 48.8 %reduce-scatter.15.cloned.1.call-done = bf16[2048,512]{1,0:T(8,128)(2,1)} async-done(((bf16[2048,1024]{1,0:T(8,128)(2,1)}), bf16[2048,512]{1,0:T(8,128)(2,1)}) %reduce-scatter.15.cloned.1.call-update) | async-done | bytes 2097168 | tf_op jit(solution)/shard_map/reduce_scatter | solution.py:42
  1184.2 59.9 %all-reduce = (f32[512]{0:T(512)}, f32[512]{0:T(512)}, f32[512]{0:T(512)}, f32[512]{0:T(512)}, f32[512]{0:T(512)}, /*index=5*/f32[512]{0:T(512)}, f32[512]{0:T(512)}, f32[2048]{0:T(1024)}, f32[512]{0:T(512)}) all-reduce(f32[512]{0:T(512)S(1)} %get-tuple-element.228, ...), channel_id=1, replica_groups=mesh['dp'=4,'row'=4,'col'=2] {'dp','row'}, use_global_device_ids=true, to_apply=%region_28.29 | all-reduce | flops 6144 | bytes 49152 | tf_op jit(solution)/shard_map/psum | solution.py:208
  (283 shorter events, 350.1 us)
Async XLA Ops:
  7.2 81.4 %all-gather.8.cloned.1.call-start = ((), (), s32[]{:S(2)}) async-start(), calls=%async_computation.8 | async-start | bytes 6291456 | tf_op jit(solution)/shard_map/all_gather | solution.py:38
  12.6 15.2 %copy-start.27 = (f32[512]{0:T(512)S(1)}, f32[512]{0:T(512)}, u32[]{:S(2)}) copy-start(f32[512]{0:T(512)} %param.23) | copy-start | bytes 6148
  31.5 122.2 %all-gather.10.cloned.1.call-start = ((), (), s32[]{:S(2)}) async-start(), calls=%async_computation.9 | async-start | bytes 3932160 | tf_op jit(solution)/shard_map/all_gather | solution.py:135
  32.2 225.5 %all-gather.12.cloned.1.call-start = ((), (), s32[]{:S(2)}) async-start(), calls=%async_computation.10 | async-start | bytes 1310720 | tf_op jit(solution)/shard_map/all_gather | solution.py:137
  32.9 330.2 %reduce-scatter.9.cloned.1.call-start = ((), (), s32[]{:S(2)}) async-start(), calls=%async_computation.11 | async-start | bytes 12582912 | tf_op jit(solution)/shard_map/reduce_scatter | solution.py:158
  33.2 130.3 %copy-start.4 = (bf16[4,512,8,64]{1,3,2,0:T(8,128)(2,1)}, bf16[4,512,8,64]{1,3,2,0:T(8,128)(2,1)S(1)}, u32[]{:S(2)}) copy-start(bf16[4,512,8,64]{1,3,2,0:T(8,128)(2,1)S(1)} %fusion.101) | copy-start | bytes 6291460
  265.2 171.3 %all-gather.18.cloned.1.call-start = ((), (), s32[]{:S(2)}) async-start(), calls=%async_computation.15 | async-start | bytes 6291456 | tf_op jit(solution)/shard_map/all_gather | solution.py:179
  270.6 92.5 %copy-start.32 = (f32[512]{0:T(512)S(1)}, f32[512]{0:T(512)}, u32[]{:S(2)}) copy-start(f32[512]{0:T(512)} %param.28) | copy-start | bytes 6148
  274.5 229.6 %all-gather.16.cloned.1.call-start = ((), (), s32[]{:S(2)}) async-start(), calls=%async_computation.13 | async-start | bytes 5242880 | tf_op jit(solution)/shard_map/all_gather | solution.py:138
  275.1 101.1 %copy-start.20 = (f32[512]{0:T(512)S(1)}, f32[512]{0:T(512)}, u32[]{:S(2)}) copy-start(f32[512]{0:T(512)} %param.29) | copy-start | bytes 6148
  275.1 101.1 %copy-start.28 = (f32[512]{0:T(512)S(1)}, f32[512]{0:T(512)}, u32[]{:S(2)}) copy-start(f32[512]{0:T(512)} %param.30) | copy-start | bytes 6148
  275.1 285.6 %all-gather.14.cloned.1.call-start = ((), (), s32[]{:S(2)}) async-start(), calls=%async_computation.12 | async-start | bytes 6291456 | tf_op jit(solution)/shard_map/all_gather | solution.py:38
  275.2 108.7 %collective-permute-start = (bf16[256,2048]{1,0:T(8,128)(2,1)S(1)}, bf16[256,2048]{1,0:T(8,128)(2,1)S(1)}, u32[]{:S(2)}, u32[]{:S(2)}) collective-permute-start(bf16[256,2048]{1,0:T(8,128)(2,1)S(1)} %copy-done.13), channel_id=1, source_target_pairs={{0,2},{2,4},{4,6},{6,0},{1,3},{3,5},{5,7},{7,1},{8,10},{10,12},{12... | collective-permute-start | bytes 3145736 | tf_op jit(solution)/shard_map/ppermute | solution.py:124
  380.2 276.7 %reduce-scatter.13.cloned.1.call-start = ((), (), s32[]{:S(2)}) async-start(), calls=%async_computation.16 | async-start | bytes 6291456 | tf_op jit(solution)/shard_map/reduce_scatter | solution.py:42
  380.3 27.2 %collective-permute-start.2 = (bf16[256,2048]{1,0:T(8,128)(2,1)S(1)}, bf16[256,2048]{1,0:T(8,128)(2,1)S(1)}, u32[]{:S(2)}, u32[]{:S(2)}) collective-permute-start(bf16[256,2048]{1,0:T(8,128)(2,1)S(1)} %copy-done.13), channel_id=1, source_target_pairs={{2,0},{4,2},{6,4},{0,6},{3,1},{5,3},{7,5},{1,7},{10,8},{12,10},{14... | collective-permute-start | bytes 3145736 | tf_op jit(solution)/shard_map/ppermute | solution.py:126
  383.9 44.0 %collective-permute-start.1 = (bf16[256,2048]{1,0:T(8,128)(2,1)S(1)}, bf16[256,2048]{1,0:T(8,128)(2,1)}, u32[]{:S(2)}, u32[]{:S(2)}) collective-permute-start(bf16[256,2048]{1,0:T(8,128)(2,1)S(1)} %collective-permute-done), channel_id=1, source_target_pairs={{0,2},{2,4},{4,6},{6,0},{1,3},{3,5},{5,7},{7,1},{8,10},{10,12},{12... | collective-permute-start | bytes 3145736 | tf_op jit(solution)/shard_map/ppermute | solution.py:124
  436.4 124.3 %copy-start.35 = (f32[2048]{0:T(1024)S(1)}, f32[2048]{0:T(1024)}, u32[]{:S(2)}) copy-start(f32[2048]{0:T(1024)} %param.32) | copy-start | bytes 24580
  560.7 30.4 %copy-start.12 = (bf16[4,256,2048]{2,1,0:T(8,128)(2,1)S(1)}, bf16[4,256,2048]{2,1,0:T(8,128)(2,1)}, u32[]{:S(2)}) copy-start(bf16[4,256,2048]{2,1,0:T(8,128)(2,1)} %gather_fusion) | copy-start | bytes 12582916
  602.4 111.8 %reduce-scatter.11.cloned.1.call-start = ((), (), s32[]{:S(2)}) async-start(), calls=%async_computation.14 | async-start | bytes 6291456 | tf_op jit(solution)/shard_map/reduce_scatter | solution.py:173
  616.3 97.9 %copy-start.29 = (f32[512]{0:T(512)S(1)}, f32[512]{0:T(512)}, u32[]{:S(2)}) copy-start(f32[512]{0:T(512)} %param.34) | copy-start | bytes 6148
  616.3 166.7 %all-gather.20.cloned.1.call-start = ((), (), s32[]{:S(2)}) async-start(), calls=%async_computation.17 | async-start | bytes 6291456 | tf_op jit(solution)/shard_map/all_gather | solution.py:190
  656.9 57.3 %copy-start.8 = (bf16[2048,512]{1,0:T(8,128)(2,1)S(1)}, bf16[2048,512]{1,0:T(8,128)(2,1)}, u32[]{:S(2)}) copy-start(bf16[2048,512]{1,0:T(8,128)(2,1)} %reduce-scatter.13.cloned.1.call-done) | copy-start | bytes 6291460
  726.1 235.3 %reduce-scatter.21.cloned.1.call-start = ((), (), s32[]{:S(2)}) async-start(), calls=%async_computation.21 | async-start | bytes 5242880 | tf_op jit(solution)/shard_map/reduce_scatter | solution.py:233
  740.3 221.1 %reduce-scatter.23.cloned.1.call-start = ((), (), s32[]{:S(2)}) async-start(), calls=%async_computation.22 | async-start | bytes 5242880 | tf_op jit(solution)/shard_map/reduce_scatter | solution.py:239
  754.4 28.6 %copy-start.34 = (bf16[512,1024]{1,0:T(8,128)(2,1)S(1)}, bf16[512,1024]{1,0:T(8,128)(2,1)}, u32[]{:S(2)}) copy-start(bf16[512,1024]{1,0:T(8,128)(2,1)} %all-gather.12.cloned.1.call-done) | copy-start | bytes 3145732
  754.4 217.9 %reduce-scatter.19.cloned.1.call-start = ((), (), s32[]{:S(2)}) async-start(), calls=%async_computation.20 | async-start | bytes 1310720 | tf_op jit(solution)/shard_map/reduce_scatter | solution.py:236
  928.0 106.0 %reduce-scatter.17.cloned.1.call-start = ((), (), s32[]{:S(2)}) async-start(), calls=%async_computation.19 | async-start | bytes 3932160 | tf_op jit(solution)/shard_map/reduce_scatter | solution.py:230
  961.3 144.1 %all-reduce.8.cloned.1.call-start = ((), (), s32[]{:S(2)}) async-start(), calls=%async_computation.23 | async-start | bytes 6291456 | tf_op jit(solution)/shard_map/psum | solution.py:224
  1034.0 128.0 %reduce-scatter.15.cloned.1.call-start = ((), (), s32[]{:S(2)}) async-start(), calls=%async_computation.18 | async-start | bytes 6291456 | tf_op jit(solution)/shard_map/reduce_scatter | solution.py:42
  1105.5 56.6 %copy-start.17 = (f32[2048]{0:T(1024)S(1)}, f32[2048]{0:T(1024)}, u32[]{:S(2)}) copy-start(f32[2048]{0:T(1024)} %copy-done.16) | copy-start | bytes 24580
  1105.5 56.6 %copy-start.19 = (f32[2048]{0:T(1024)S(1)}, f32[2048]{0:T(1024)}, u32[]{:S(2)}) copy-start(f32[2048]{0:T(1024)} %copy-done.18) | copy-start | bytes 24580
  1105.5 56.6 %copy-start.22 = (f32[512]{0:T(512)S(1)}, f32[512]{0:T(512)}, u32[]{:S(2)}) copy-start(f32[512]{0:T(512)} %param.22) | copy-start | bytes 6148
  (38 other events, 208.1 us)
Sparse Core Ops, SparseCore 0:
  31.6 56.9 all-gather.7
  90.2 63.4 all-gather.9
  155.3 28.8 all-gather.11
  265.3 97.8 reduce-scatter.8
  365.2 56.7 all-gather.17
  423.5 80.6 all-gather.15
  505.8 54.9 all-gather.13
  602.5 54.3 reduce-scatter.12
  659.8 54.3 reduce-scatter.10
  726.2 56.7 all-gather.19
  785.4 76.7 reduce-scatter.20
  864.3 77.2 reduce-scatter.22
  944.6 27.6 reduce-scatter.18
  975.0 58.8 reduce-scatter.16
  1036.4 68.9 all-reduce.7
  1107.6 54.3 reduce-scatter.14
